TPU v7x, 512 devices: a whole 4x8x8 slice. The times are simulated.
512 devices in a mesh: resp: 8 (over z), fsdp: 16 (over y, core), head: 4 (over x).
Axes of the slice: x: 4, y: 8, z: 8, core: 2. Of those that a mesh axis runs over, the one named last changes fastest.
Arguments:
- queries: bfloat16 [32768, 4096], P(('resp', 'fsdp'), 'head'), may hold values from -12 to 12
- self_keys: bfloat16 [32768, 512], P(('resp', 'fsdp'), 'head'), may hold values from -12 to 12
- self_values: bfloat16 [32768, 512], P(('resp', 'fsdp'), 'head'), may hold values from -6 to 6
- d_out: bfloat16 [32768, 4096], P(('resp', 'fsdp'), 'head'), may hold values from -12 to 12
- prompt_keys: bfloat16 [16, 256, 512], P('resp', 'fsdp', 'head'), may hold values from -6 to 6
- prompt_values: bfloat16 [16, 256, 512], P('resp', 'fsdp', 'head'), may hold values from -6 to 6
- counts: int32 [16], replicated, may hold values from 1 to 16, 128 in all
- owner_slot: int32 [16], replicated, may hold values from 0 to 15, each once
- prompt_blocks: int32 [16], replicated, may hold values from 1 to 2
- resp_blocks: int32 [128], P(('resp', 'fsdp')), may hold values from 1 to 2
- grad_q: bfloat16 [8192, 4096], P('fsdp', ('resp', 'head')), may hold values from -4 to 4
- momentum: float32 [8192, 4096], P('fsdp', ('resp', 'head')), may hold values from -30 to 30
- basis: float32 [4096, 256], P(('resp', 'head')), may hold values from -0.09375 to 0.09375
Outputs:
- dq: bfloat16 [32768, 4096], P(('resp', 'fsdp'), 'head')
- resp_kv_grad: bfloat16 [2, 32768, 512], P(None, ('resp', 'fsdp'), 'head')
- prompt_kv_grad: float32 [2, 16, 256, 512], P(None, 'resp', 'fsdp', 'head')
- update: bfloat16 [8192, 4096], P('fsdp', ('resp', 'head'))
- momentum_out: float32 [8192, 4096], P('fsdp', ('resp', 'head'))
- basis_out: float32 [4096, 256], P(('resp', 'head'))
Inputs may be any that keep to these rules, and one draw needn't show every extreme that they name: `counts`: responses are stored group by group in the order of the groups. `owner_slot`: each row of prompt_keys holds the prompt of exactly one group.
All inputs are finite; a program needn't handle non-finite values.
Results may differ from a plain program's by a relative error of at most 0.0087.
Values may be sent and summed in bfloat16 or wider, within the bound.
A program may use at most 64 MiB of HBM per device.

v0:
```python
import math

import jax
import jax.numpy as jnp
from jax import lax
from jax.sharding import PartitionSpec as P

D = 8192
HD = 128
QCOLS = 4096
RANK = 256


momentum_keep = 0.95
norm_eps = 1e-06


def combined_all(value, axis, combine):
    everything = lax.all_gather(value, axis)
    initial = everything[0]

    def step(k, so_far):
        return combine(so_far, everything[k])

    return lax.fori_loop(1, lax.axis_size(axis), step, initial)


def group_index(counts, order):
    ends = jnp.cumsum(counts)
    return jnp.sum((ends[None, :] <= order[:, None]).astype(jnp.int32), axis=1)


def key_mask(height, width, prompt_len, prompt_cap, resp_len):
    place = jnp.arange(width, dtype=jnp.int32)[None, :]
    position = jnp.arange(height, dtype=jnp.int32)[:, None]
    inner = place - prompt_cap
    return jnp.where(
        place < prompt_cap, place < prompt_len, (inner <= position) & (inner < resp_len)
    )


def attend_group(q_part, o_grad, keys, values, prompt_len, prompt_cap, resp_len):
    height = q_part.shape[0]
    depth = q_part.shape[2]
    scale = depth ** (-0.5)
    raw = jnp.einsum("thd,kd->htk", q_part, keys, preferred_element_type=jnp.float32) * scale
    visible = key_mask(height, keys.shape[0], prompt_len, prompt_cap, resp_len)
    logits = jnp.where(visible[None], raw, -jnp.inf)
    peak = jnp.max(logits, axis=2, keepdims=True)
    lse = peak + jnp.log(jnp.sum(jnp.exp(logits - peak), axis=2, keepdims=True))
    weight = jnp.exp(logits - lse).astype(jnp.bfloat16)
    output = jnp.einsum("htk,kd->htd", weight, values, preferred_element_type=jnp.float32)
    diag = jnp.sum(jnp.swapaxes(o_grad.astype(jnp.float32), 0, 1) * output, axis=2)
    p_grad = jnp.einsum("thd,kd->htk", o_grad, values, preferred_element_type=jnp.float32)
    s_grad = (weight.astype(jnp.float32) * (p_grad - diag[..., None])).astype(jnp.bfloat16)
    q_grad = jnp.einsum("htk,kd->thd", s_grad, keys, preferred_element_type=jnp.float32)
    k_grads = jnp.einsum("htk,thd->kd", s_grad, q_part, preferred_element_type=jnp.float32) * scale
    v_grads = jnp.einsum("htk,thd->kd", weight, o_grad, preferred_element_type=jnp.float32)
    return (q_grad * scale, k_grads, v_grads)


def on_device(
    queries,
    self_keys,
    self_values,
    d_out,
    prompt_keys,
    prompt_values,
    counts,
    owner_slot,
    prompt_blocks,
    resp_blocks,
    grad_q,
    momentum,
    basis,
):
    highest = lax.Precision.HIGHEST
    fsdp_count = lax.axis_size("fsdp")
    row_index = lax.axis_index("resp")
    col_index = lax.axis_index("fsdp")
    piece = prompt_keys.shape[1]
    kv_cols = prompt_keys.shape[2]
    prompt_cap = piece * fsdp_count
    height = queries.shape[0]
    my_group = group_index(counts, jnp.reshape(row_index * fsdp_count + col_index, (1,)))[0]
    prompt_len = prompt_blocks[my_group] * 128
    resp_len = resp_blocks[0] * 128
    stacked = jnp.stack([prompt_keys, prompt_values], 0)
    everyone = lax.all_gather(stacked, "resp", axis=1, tiled=True)
    row_slots = owner_slot[
        group_index(counts, row_index * fsdp_count + jnp.arange(fsdp_count, dtype=jnp.int32))
    ]
    outgoing = jnp.take(everyone, row_slots, axis=1)
    arrived = lax.all_to_all(outgoing, "fsdp", split_axis=1, concat_axis=2, tiled=True)
    prompt_kv = arrived.reshape(2, prompt_cap, kv_cols)
    live = jnp.arange(height, dtype=jnp.int32) < resp_len
    masked_grad = jnp.where(live[:, None], d_out, jnp.zeros((), jnp.bfloat16))
    keys_all = jnp.concatenate([prompt_kv[0], self_keys], 0)
    values_all = jnp.concatenate([prompt_kv[1], self_values], 0)
    per_group = queries.shape[1] // self_keys.shape[1]
    q_part = queries.reshape(height, per_group, HD)
    o_part = masked_grad.reshape(height, per_group, HD)
    q_grad, k_grad, v_grad = attend_group(
        q_part, o_part, keys_all, values_all, prompt_len, prompt_cap, resp_len
    )
    q_parts = q_grad.reshape(height, per_group * HD)
    k_parts = k_grad
    v_parts = v_grad
    dq = q_parts.astype(jnp.bfloat16)
    k_grad = k_parts
    v_grad = v_parts
    resp_grad = jnp.stack([k_grad[prompt_cap:], v_grad[prompt_cap:]], 0).astype(jnp.bfloat16)
    partial_value = jnp.stack([k_grad[:prompt_cap], v_grad[:prompt_cap]], 0).reshape(
        2, fsdp_count, piece, kv_cols
    )
    returned = lax.all_to_all(partial_value, "fsdp", split_axis=1, concat_axis=1, tiled=True)
    chooser = (row_slots[None, :] == jnp.arange(counts.shape[0], dtype=jnp.int32)[:, None]).astype(
        jnp.float32
    )
    by_slot = jnp.einsum("sf,afpc->aspc", chooser, returned, precision=highest)
    prompt_grad = lax.psum_scatter(by_slot, "resp", scatter_dimension=1, tiled=True)
    total = momentum + grad_q.astype(jnp.float32)
    projected = lax.psum(jnp.dot(total, basis, precision=highest), ("resp", "head"))
    gram = jnp.dot(projected.T, projected, precision=highest)

    def join(former, latter):
        summed = jnp.dot(former.T, former, precision=highest) + jnp.dot(
            latter.T, latter, precision=highest
        )
        return jnp.linalg.cholesky(summed).T

    upper = combined_all(jnp.linalg.cholesky(gram).T, "fsdp", join)
    lower = upper.T
    ortho = jax.scipy.linalg.solve_triangular(lower, projected.T, lower=True).T
    back = lax.psum(jnp.dot(total.T, ortho, precision=highest), "fsdp")
    momentum_out = total - (1.0 - momentum_keep) * jnp.dot(ortho, back.T, precision=highest)
    squares = lax.psum(jnp.sum(back * back, axis=0), ("resp", "head"))
    basis_out = back * lax.rsqrt(squares + norm_eps)
    update = (math.sqrt(D * QCOLS / RANK) * jnp.dot(ortho, basis_out.T, precision=highest)).astype(
        jnp.bfloat16
    )
    return (dq, resp_grad, prompt_grad, update, momentum_out, basis_out)


def solution(mesh):
    placed = (
        P(("resp", "fsdp"), "head"),
        P(("resp", "fsdp"), "head"),
        P(("resp", "fsdp"), "head"),
        P(("resp", "fsdp"), "head"),
        P("resp", "fsdp", "head"),
        P("resp", "fsdp", "head"),
        P(),
        P(),
        P(),
        P(("resp", "fsdp")),
        P("fsdp", ("resp", "head")),
        P("fsdp", ("resp", "head")),
        P(("resp", "head"), None),
    )
    return jax.shard_map(
        on_device,
        mesh=mesh,
        in_specs=placed,
        out_specs=(
            P(("resp", "fsdp"), "head"),
            P(None, ("resp", "fsdp"), "head"),
            P(None, "resp", "fsdp", "head"),
            P("fsdp", ("resp", "head")),
            P("fsdp", ("resp", "head")),
            P(("resp", "head"), None),
        ),
        check_vma=False,
    )
```

profile of v0, /device:TPU:32, one launch (start us, length us, event | category | flops | bytes accessed | tf_op | source)
XLA Modules:
  0.0 1086.4 jit_solution(14902609720798085587)
XLA Ops:
  10.7 166.9 %all-reduce.4.cloned.1.call-done = f32[512,256]{1,0:T(8,128)} async-done(((f32[512,256]{1,0:T(8,128)}), f32[512,256]{1,0:T(8,128)}) %all-reduce.4.cloned.1.call-update) | async-done | bytes 524304 | tf_op jit(solution)/shard_map/psum | solution.py:123
  180.0 11.7 %cholesky.164 = f32[128,128]{1,0:T(8,128)S(1)} custom-call(f32[128,128]{1,0:T(8,128)S(1)} %cholesky.197), custom_call_target="Cholesky" | custom-call | tf_op jit(solution)/shard_map/jit(cholesky)/cholesky | solution.py:132
  202.1 11.7 %cholesky.181 = f32[128,128]{1,0:T(8,128)S(1)} custom-call(f32[128,128]{1,0:T(8,128)S(1)} %convolution_subtract_fusion.2), custom_call_target="Cholesky" | custom-call | tf_op jit(solution)/shard_map/jit(cholesky)/cholesky | solution.py:132
  218.2 24.6 %all_gather.9 = bf16[2,16,16,128]{3,2,1,0:T(8,128)(2,1)S(1)} all-gather(bf16[2,2,16,128]{3,2,1,0:T(8,128)(2,1)S(1)} %pad_maximum_fusion.6), channel_id=1, replica_groups=mesh['resp'=8,'fsdp'=16,'head'=4] {'resp'}, dimensions={1}, use_global_device_ids=true | all-gather | bytes 147456 | tf_op jit(solution)/shard_map/all_gather | solution.py:89
  285.9 571.1 %while.16 = (s32[]{:T(128)}, f32[256,256]{0,1:T(8,128)S(1)}, f32[16,256,256]{2,1,0:T(8,128)}, s32[]{:T(128)}, s32[]{:T(128)}, /*index=5*/s32[]{:T(128)}, f32[]{:T(128)}) while((s32[]{:T(128)}, f32[256,256]{0,1:T(8,128)S(1)}, f32[16,256,256]{2,1,0:T(8,128)}, s32[]{:T(128)}, s32[]{:T(128)}, /*index=5*/s32[]{:T(128)}, f32[]{:T(128)}) %tuple.98), condition=%wide.region_13.15_spmd, body=%wide.region_12.14_spmd.sunk | while | flops 453525760 | bytes 4393093 | solution.py:25
  288.1 11.7 %cholesky.347 = f32[128,128]{1,0:T(8,128)S(1)} custom-call(f32[128,128]{1,0:T(8,128)S(1)} %cholesky.346), custom_call_target="Cholesky" | custom-call | tf_op jit(solution)/shard_map/while/body/eval_jaxpr/jit(cholesky)/cholesky | solution.py:130
  310.2 11.7 %cholesky.349 = f32[128,128]{1,0:T(8,128)S(1)} custom-call(f32[128,128]{1,0:T(8,128)S(1)} %convolution_subtract_fusion.4), custom_call_target="Cholesky" | custom-call | tf_op jit(solution)/shard_map/while/body/eval_jaxpr/jit(cholesky)/cholesky | solution.py:130
  326.2 11.7 %cholesky.347 = f32[128,128]{1,0:T(8,128)S(1)} custom-call(f32[128,128]{1,0:T(8,128)S(1)} %cholesky.346), custom_call_target="Cholesky" | custom-call | tf_op jit(solution)/shard_map/while/body/eval_jaxpr/jit(cholesky)/cholesky | solution.py:130
  348.3 11.7 %cholesky.349 = f32[128,128]{1,0:T(8,128)S(1)} custom-call(f32[128,128]{1,0:T(8,128)S(1)} %convolution_subtract_fusion.4), custom_call_target="Cholesky" | custom-call | tf_op jit(solution)/shard_map/while/body/eval_jaxpr/jit(cholesky)/cholesky | solution.py:130
  364.3 11.7 %cholesky.347 = f32[128,128]{1,0:T(8,128)S(1)} custom-call(f32[128,128]{1,0:T(8,128)S(1)} %cholesky.346), custom_call_target="Cholesky" | custom-call | tf_op jit(solution)/shard_map/while/body/eval_jaxpr/jit(cholesky)/cholesky | solution.py:130
  386.4 11.7 %cholesky.349 = f32[128,128]{1,0:T(8,128)S(1)} custom-call(f32[128,128]{1,0:T(8,128)S(1)} %convolution_subtract_fusion.4), custom_call_target="Cholesky" | custom-call | tf_op jit(solution)/shard_map/while/body/eval_jaxpr/jit(cholesky)/cholesky | solution.py:130
  402.4 11.7 %cholesky.347 = f32[128,128]{1,0:T(8,128)S(1)} custom-call(f32[128,128]{1,0:T(8,128)S(1)} %cholesky.346), custom_call_target="Cholesky" | custom-call | tf_op jit(solution)/shard_map/while/body/eval_jaxpr/jit(cholesky)/cholesky | solution.py:130
  424.5 11.7 %cholesky.349 = f32[128,128]{1,0:T(8,128)S(1)} custom-call(f32[128,128]{1,0:T(8,128)S(1)} %convolution_subtract_fusion.4), custom_call_target="Cholesky" | custom-call | tf_op jit(solution)/shard_map/while/body/eval_jaxpr/jit(cholesky)/cholesky | solution.py:130
  440.5 11.7 %cholesky.347 = f32[128,128]{1,0:T(8,128)S(1)} custom-call(f32[128,128]{1,0:T(8,128)S(1)} %cholesky.346), custom_call_target="Cholesky" | custom-call | tf_op jit(solution)/shard_map/while/body/eval_jaxpr/jit(cholesky)/cholesky | solution.py:130
  462.6 11.7 %cholesky.349 = f32[128,128]{1,0:T(8,128)S(1)} custom-call(f32[128,128]{1,0:T(8,128)S(1)} %convolution_subtract_fusion.4), custom_call_target="Cholesky" | custom-call | tf_op jit(solution)/shard_map/while/body/eval_jaxpr/jit(cholesky)/cholesky | solution.py:130
  478.6 11.7 %cholesky.347 = f32[128,128]{1,0:T(8,128)S(1)} custom-call(f32[128,128]{1,0:T(8,128)S(1)} %cholesky.346), custom_call_target="Cholesky" | custom-call | tf_op jit(solution)/shard_map/while/body/eval_jaxpr/jit(cholesky)/cholesky | solution.py:130
  500.6 11.7 %cholesky.349 = f32[128,128]{1,0:T(8,128)S(1)} custom-call(f32[128,128]{1,0:T(8,128)S(1)} %convolution_subtract_fusion.4), custom_call_target="Cholesky" | custom-call | tf_op jit(solution)/shard_map/while/body/eval_jaxpr/jit(cholesky)/cholesky | solution.py:130
  516.6 11.7 %cholesky.347 = f32[128,128]{1,0:T(8,128)S(1)} custom-call(f32[128,128]{1,0:T(8,128)S(1)} %cholesky.346), custom_call_target="Cholesky" | custom-call | tf_op jit(solution)/shard_map/while/body/eval_jaxpr/jit(cholesky)/cholesky | solution.py:130
  538.7 11.7 %cholesky.349 = f32[128,128]{1,0:T(8,128)S(1)} custom-call(f32[128,128]{1,0:T(8,128)S(1)} %convolution_subtract_fusion.4), custom_call_target="Cholesky" | custom-call | tf_op jit(solution)/shard_map/while/body/eval_jaxpr/jit(cholesky)/cholesky | solution.py:130
  554.7 11.7 %cholesky.347 = f32[128,128]{1,0:T(8,128)S(1)} custom-call(f32[128,128]{1,0:T(8,128)S(1)} %cholesky.346), custom_call_target="Cholesky" | custom-call | tf_op jit(solution)/shard_map/while/body/eval_jaxpr/jit(cholesky)/cholesky | solution.py:130
  576.8 11.7 %cholesky.349 = f32[128,128]{1,0:T(8,128)S(1)} custom-call(f32[128,128]{1,0:T(8,128)S(1)} %convolution_subtract_fusion.4), custom_call_target="Cholesky" | custom-call | tf_op jit(solution)/shard_map/while/body/eval_jaxpr/jit(cholesky)/cholesky | solution.py:130
  592.8 11.7 %cholesky.347 = f32[128,128]{1,0:T(8,128)S(1)} custom-call(f32[128,128]{1,0:T(8,128)S(1)} %cholesky.346), custom_call_target="Cholesky" | custom-call | tf_op jit(solution)/shard_map/while/body/eval_jaxpr/jit(cholesky)/cholesky | solution.py:130
  614.8 11.7 %cholesky.349 = f32[128,128]{1,0:T(8,128)S(1)} custom-call(f32[128,128]{1,0:T(8,128)S(1)} %convolution_subtract_fusion.4), custom_call_target="Cholesky" | custom-call | tf_op jit(solution)/shard_map/while/body/eval_jaxpr/jit(cholesky)/cholesky | solution.py:130
  652.9 11.7 %cholesky.349 = f32[128,128]{1,0:T(8,128)S(1)} custom-call(f32[128,128]{1,0:T(8,128)S(1)} %convolution_subtract_fusion.4), custom_call_target="Cholesky" | custom-call | tf_op jit(solution)/shard_map/while/body/eval_jaxpr/jit(cholesky)/cholesky | solution.py:130
  691.0 11.7 %cholesky.349 = f32[128,128]{1,0:T(8,128)S(1)} custom-call(f32[128,128]{1,0:T(8,128)S(1)} %convolution_subtract_fusion.4), custom_call_target="Cholesky" | custom-call | tf_op jit(solution)/shard_map/while/body/eval_jaxpr/jit(cholesky)/cholesky | solution.py:130
  729.1 11.7 %cholesky.349 = f32[128,128]{1,0:T(8,128)S(1)} custom-call(f32[128,128]{1,0:T(8,128)S(1)} %convolution_subtract_fusion.4), custom_call_target="Cholesky" | custom-call | tf_op jit(solution)/shard_map/while/body/eval_jaxpr/jit(cholesky)/cholesky | solution.py:130
  767.1 11.7 %cholesky.349 = f32[128,128]{1,0:T(8,128)S(1)} custom-call(f32[128,128]{1,0:T(8,128)S(1)} %convolution_subtract_fusion.4), custom_call_target="Cholesky" | custom-call | tf_op jit(solution)/shard_map/while/body/eval_jaxpr/jit(cholesky)/cholesky | solution.py:130
  805.2 11.7 %cholesky.349 = f32[128,128]{1,0:T(8,128)S(1)} custom-call(f32[128,128]{1,0:T(8,128)S(1)} %convolution_subtract_fusion.4), custom_call_target="Cholesky" | custom-call | tf_op jit(solution)/shard_map/while/body/eval_jaxpr/jit(cholesky)/cholesky | solution.py:130
  843.3 11.7 %cholesky.349 = f32[128,128]{1,0:T(8,128)S(1)} custom-call(f32[128,128]{1,0:T(8,128)S(1)} %convolution_subtract_fusion.4), custom_call_target="Cholesky" | custom-call | tf_op jit(solution)/shard_map/while/body/eval_jaxpr/jit(cholesky)/cholesky | solution.py:130
  862.3 20.6 %custom-call.12 = f32[2,128,128]{1,2,0:T(8,128)S(1)} custom-call(f32[2,128,128]{2,1,0:T(8,128)} %get-tuple-element.103), custom_call_target="InvertDiagBlocksLowerTriangular" | custom-call | tf_op jit(solution)/shard_map/jit(_solve_triangular)/triangular_solve | solution.py:134
  887.8 109.5 %all-reduce.6.cloned.1.call-done = f32[128,256]{1,0:T(8,128)} async-done(((f32[128,256]{1,0:T(8,128)}), f32[128,256]{1,0:T(8,128)}) %all-reduce.6.cloned.1.call-update) | async-done | bytes 131088 | tf_op jit(solution)/shard_map/psum | solution.py:135
  998.2 75.7 %psum.23 = f32[256]{0:T(256)S(1)} all-reduce(f32[256]{0:T(256)S(1)} %multiply_reduce_fusion), channel_id=1, replica_groups=mesh['resp'=8,'fsdp'=16,'head'=4] {'resp','head'}, use_global_device_ids=true, to_apply=%region_16.18 | all-reduce | flops 256 | bytes 2048 | tf_op jit(solution)/shard_map/psum | solution.py:137
  (323 shorter events, 348.5 us)
Async XLA Ops:
  8.0 248.3 %copy-start = (bf16[256,1024]{1,0:T(8,128)(2,1)S(1)}, bf16[256,1024]{1,0:T(8,128)(2,1)}, u32[]{:S(2)}) copy-start(bf16[256,1024]{1,0:T(8,128)(2,1)} %param.16) | copy-start | bytes 1572868
  8.0 208.5 %copy-start.13 = (s32[16]{0:T(128)S(1)}, s32[16]{0:T(128)}, u32[]{:S(2)}) copy-start(s32[16]{0:T(128)} %param.22) | copy-start | bytes 196
  8.0 209.5 %copy-start.1 = (s32[16]{0:T(128)S(1)}, s32[16]{0:T(128)}, u32[]{:S(2)}) copy-start(s32[16]{0:T(128)} %param.23) | copy-start | bytes 196
  8.0 210.2 %copy-start.12 = (bf16[2,16,128]{2,1,0:T(8,128)(2,1)S(1)}, bf16[2,16,128]{2,1,0:T(8,128)(2,1)}, u32[]{:S(2)}) copy-start(bf16[2,16,128]{2,1,0:T(8,128)(2,1)} %param.20) | copy-start | bytes 24580
  8.0 210.2 %copy-start.11 = (bf16[2,16,128]{2,1,0:T(8,128)(2,1)S(1)}, bf16[2,16,128]{2,1,0:T(8,128)(2,1)}, u32[]{:S(2)}) copy-start(bf16[2,16,128]{2,1,0:T(8,128)(2,1)} %param.21) | copy-start | bytes 24580
  8.1 245.9 %copy-start.14 = (s32[16]{0:T(128)S(1)}, s32[16]{0:T(128)}, u32[]{:S(2)}) copy-start(s32[16]{0:T(128)} %param.24) | copy-start | bytes 196
  8.1 247.2 %copy-start.6 = (bf16[256,1024]{1,0:T(8,128)(2,1)S(1)}, bf16[256,1024]{1,0:T(8,128)(2,1)}, u32[]{:S(2)}) copy-start(bf16[256,1024]{1,0:T(8,128)(2,1)} %param.19) | copy-start | bytes 1572868
  8.1 169.6 %all-reduce.4.cloned.1.call-start = ((), (), s32[]{:S(2)}) async-start(), calls=%async_computation.4 | async-start | bytes 1048576 | tf_op jit(solution)/shard_map/psum | solution.py:123
  10.7 245.6 %copy-start.8 = (bf16[256,128]{1,0:T(8,128)(2,1)S(1)}, bf16[256,128]{1,0:T(8,128)(2,1)}, u32[]{:S(2)}) copy-start(bf16[256,128]{1,0:T(8,128)(2,1)} %param.17) | copy-start | bytes 196612
  10.7 269.5 %all-gather.3.cloned.1.call-start = ((), (), s32[]{:S(2)}) async-start(), calls=%async_computation.6 | async-start | bytes 4456448 | tf_op jit(solution)/shard_map/all_gather | solution.py:19
  244.2 12.1 %all-to-all-start = ((bf16[2,16,16,128]{3,2,0,1:T(8,128)(2,1)}), bf16[2,16,16,128]{3,2,0,1:T(8,128)(2,1)S(1)}, u32[]{:S(2)}, u32[]{:S(2)}) async-start(bf16[2,16,16,128]{3,2,0,1:T(8,128)(2,1)} %select_bitcast_fusion.3), calls=%async_computation | async-start | bytes 262144 | tf_op jit(solution)/shard_map/all_to_all | solution.py:94
  257.9 0.9 copy-start.10
  260.7 0.7 copy-start.9
  262.2 0.7 copy-start.5
  263.6 15.3 %all-to-all-start.1 = ((f32[2,16,16,128]{3,2,0,1:T(8,128)}), f32[2,16,16,128]{3,2,0,1:T(8,128)S(1)}, u32[]{:S(2)}, u32[]{:S(2)}) async-start(f32[2,16,16,128]{3,2,0,1:T(8,128)} %pad_maximum_fusion.4), calls=%async_computation.1 | async-start | bytes 524288 | tf_op jit(solution)/shard_map/all_to_all | solution.py:116
  271.5 614.9 %reduce-scatter.2.cloned.1.call-start = ((), (), s32[]{:S(2)}) async-start(), calls=%async_computation.3 | async-start | bytes 294912 | tf_op jit(solution)/shard_map/reduce_scatter | solution.py:121
  280.1 717.2 %all-reduce.6.cloned.1.call-start = ((), (), s32[]{:S(2)}) async-start(), calls=%async_computation.5 | async-start | bytes 262144 | tf_op jit(solution)/shard_map/psum | solution.py:135
  280.2 5.7 slice-start
  285.8 597.1 %copy-start.2 = (f32[512,256]{1,0:T(8,128)S(1)}, f32[512,256]{1,0:T(8,128)}, u32[]{:S(2)}) copy-start(f32[512,256]{1,0:T(8,128)} %all-reduce.4.cloned.1.call-done) | copy-start | bytes 1572868
  285.8 598.6 %copy-start.3 = (f32[512,128]{1,0:T(8,128)S(1)}, f32[512,128]{1,0:T(8,128)}, u32[]{:S(2)}) copy-start(f32[512,128]{1,0:T(8,128)} %param.27) | copy-start | bytes 786436
  285.9 598.6 %copy-start.4 = (bf16[512,128]{1,0:T(8,128)(2,1)S(1)}, bf16[512,128]{1,0:T(8,128)(2,1)}, u32[]{:S(2)}) copy-start(bf16[512,128]{1,0:T(8,128)(2,1)} %param.26) | copy-start | bytes 393220
  1074.8 4.3 copy-start.7
Sparse Core Ops, SparseCore 0:
  12.8 164.7 all-reduce.3
  216.7 40.3 all-gather.2
  885.8 111.3 all-reduce.5
Sparse Core Ops, SparseCore 1:
  280.2 37.9 reduce-scatter.1
where the time goes:
time: 1100 us; the launch traced here: 1090 us
  other arithmetic  573 us (52%)
  waiting for transfers between devices  281 us (26%)
  blocking collectives  100 us (9%)
  matrix products  54.1 us (5%)
  local copies, waits for them, and re-layouts  22 us (2%)
  loops' own time  20.9 us (2%)
  between operations  20.4 us (2%)
  starting transfers between devices  15.3 us (1%)
    another operation x90, other arithmetic, join(): return jnp.linalg.cholesky(summed).T  509 us
    psum x1, waiting for transfers between devices, on_device(): lax.psum(jnp.dot(total, basis, precision=highest), ('resp', 'head'))  167 us
    psum x1, waiting for transfers between devices, on_device(): back = lax.psum(jnp.dot(total.T, ortho, precision=highest), 'fsdp')  109 us
    psum x1, blocking collectives, on_device(): squares = lax.psum(jnp.sum(back * back, axis=0), ('resp', 'head'))  75.7 us
    another operation x6, other arithmetic, on_device(): upper = combined_all(jnp.linalg.cholesky(gram).T, 'fsdp', join)  34 us
    all_gather x1, blocking collectives, on_device(): everyone = lax.all_gather(stacked, 'resp', axis=1, tiled=True)  24.6 us
    dot_general x15, matrix products, join(): jnp.dot(latter.T, latter, precision=highest)  24.5 us
  transfers between devices with their start and end apart: 6, of which 4 were waited for; matrix products, arithmetic and copies ran while one was open for 55% of the time, Pallas kernels for 0%

commit v1 on v0

v1 whole, which is shorter than its diff:
```python
import math

import jax
import jax.numpy as jnp
from jax import lax
from jax.experimental import pallas as pl
from jax.experimental.pallas import tpu as pltpu
from jax.sharding import PartitionSpec as P

MESH = pl.DeviceIdType.MESH
HIGHEST = lax.Precision.HIGHEST
F32 = jnp.float32
BF16 = jnp.bfloat16

NR, NF, NH = 8, 16, 4
HD = 128
RANK = 256
GAIN = math.sqrt(8192 * 4096 / 256)
COPIES = 103


def mm(a, b, ca, cb, precision=None):
    return lax.dot_general(
        a, b, (((ca,), (cb,)), ((), ())), precision=precision, preferred_element_type=F32
    )


def exact(a, b, ca, cb):
    return mm(a, b, ca, cb, HIGHEST)


class Net:
    def __init__(self, sent, arrived):
        self.sent, self.arrived, self.n = sent, arrived, 0
        self.open = []

    def copy(self, src, dst, lands, device):
        at = self.n
        self.n += 1
        go = pltpu.make_async_remote_copy(
            src_ref=src, dst_ref=dst, send_sem=self.sent.at[at], recv_sem=self.arrived.at[at],
            device_id=device, device_id_type=MESH,
        )
        come = pltpu.make_async_remote_copy(
            src_ref=src, dst_ref=lands, send_sem=self.sent.at[at], recv_sem=self.arrived.at[at],
            device_id=device, device_id_type=MESH,
        )
        go.start()
        self.open.append(go)
        return come

    def finish(self):
        for c in self.open:
            c.wait_send()


def whole_factor(a_ref, x_ref, o_ref):
    row = lax.broadcasted_iota(jnp.int32, (8, 128), 0)
    r128 = lax.broadcasted_iota(jnp.int32, (128, 128), 0)
    c128 = lax.broadcasted_iota(jnp.int32, (128, 128), 1)
    x_ref[...] = jnp.where(r128 == c128, 1.0, 0.0).astype(F32)

    def line(v, j):
        return jnp.broadcast_to(v[j : j + 1, :], (8, 128))

    def lane(v, j):
        return jnp.broadcast_to(v[:, j : j + 1], (8, 128))

    def panel(p, carry):
        at = pl.ds(pl.multiple_of(p * 8, 8), 8)
        turn = lax.rem(128 - p * 8, 128)
        z, zx = a_ref[at, :], x_ref[at, :]
        turned = pltpu.roll(z, turn, 1)
        cols = [lane(turned, j) for j in range(8)]
        out = jnp.zeros((8, 128), F32)
        for j in range(8):
            pivot = line(cols[j], j)
            inv = 1.0 / pivot
            root = lax.rsqrt(pivot)
            root = root * (1.5 - 0.5 * pivot * root * root)
            coef = cols[j] * inv
            here = row == j
            zj, zxj = line(z, j), line(zx, j)
            out = jnp.where(here, zxj * root, out)
            z = jnp.where(here, zj * inv, z - coef * zj)
            zx = jnp.where(here, zxj * inv, zx - coef * zxj)
            for m in range(j + 1, 8):
                cm = line(cols[m], j)
                cols[m] = jnp.where(here, cm * inv, cols[m] - coef * cm)
        o_ref[at, :] = out
        zs = [line(z, j) for j in range(8)]
        zxs = [line(zx, j) for j in range(8)]
        for t in range(1, 16):
            below = jnp.where(p < t, 1.0, 0.0).astype(F32)
            a_t, x_t = a_ref[8 * t : 8 * t + 8, :], x_ref[8 * t : 8 * t + 8, :]
            turned = pltpu.roll(a_t, turn, 1) * below
            for j in range(8):
                c = lane(turned, j)
                a_t = a_t - c * zs[j]
                x_t = x_t - c * zxs[j]
            a_ref[8 * t : 8 * t + 8, :] = a_t
            x_ref[8 * t : 8 * t + 8, :] = x_t
        return carry

    lax.fori_loop(0, 16, panel, 0)


def kernel(
    q_ref, sk_ref, sv_ref, do_ref, pk_ref, pv_ref, counts_ref, owner_ref, pblk_ref, rblk_ref,
    gq_ref, mom_ref, basis_ref,
    dq_ref, kv_ref, pg_ref, upd_ref, mo_ref, bo_ref,
    total, pp, xr, xs, s1, zr, pf, gy, fr, gs, yr, gyf, evk, evv, sel, kvb, bias, gm, kt, acc,
    ret, ret_in, bys, bys_in, sqx, sqz, fa, fx, li, orth, back, sent, arrived,
):
    r, f, h = lax.axis_index("resp"), lax.axis_index("fsdp"), lax.axis_index("head")
    y, c = f // 2, f % 2
    net = Net(sent, arrived)
    right, left = (h + 1) % NH, (h + 3) % NH
    scale = HD ** -0.5

    def zpeer(d):
        return (r + d) % NR

    def fpeer(d):
        return (f + d) % NF

    def ypeer(d):
        return (y + d) % 8

    barrier = pltpu.get_barrier_semaphore()
    for d in range(1, NH):
        pl.semaphore_signal(barrier, inc=1, device_id=(r, f, (h + d) % NH), device_id_type=MESH)
    for d in range(1, NR):
        pl.semaphore_signal(barrier, inc=1, device_id=(zpeer(d), f, h), device_id_type=MESH)
    for d in range(1, NF):
        pl.semaphore_signal(barrier, inc=1, device_id=(r, fpeer(d), h), device_id_type=MESH)

    total[...] = mom_ref[...] + gq_ref[...].astype(F32)
    for k in range(8):
        pp[k] = exact(total[64 * k : 64 * k + 64, :], basis_ref[...], 1, 0)
    evk[r] = pk_ref[...]
    evv[r] = pv_ref[...]

    ends = []
    run = jnp.int32(0)
    for g in range(16):
        run = run + counts_ref[g]
        ends.append(run)

    def group_of(order):
        n = jnp.int32(0)
        for g in range(15):
            n = n + jnp.where(ends[g] <= order, 1, 0).astype(jnp.int32)
        return n

    slots = [owner_ref[group_of(r * NF + k)] for k in range(NF)]
    plen = pblk_ref[group_of(r * NF + f)] * 128
    rlen = rblk_ref[0] * 128

    pl.semaphore_wait(barrier, (NH - 1) + (NR - 1) + (NF - 1))

    opp = (h + 2) % NH
    to_r, to_l = (r, f, right), (r, f, left)
    rel_l = net.copy(pp.at[opp * 2], xr.at[0], xr.at[0], to_r)
    rel_r = net.copy(pp.at[opp * 2 + 1], xr.at[1], xr.at[1], to_l)
    ev_in = []
    for d in range(1, NR):
        src = (r + NR - d) % NR
        ev_in.append(net.copy(pk_ref, evk.at[r], evk.at[src], (zpeer(d), f, h)))
        ev_in.append(net.copy(pv_ref, evv.at[r], evv.at[src], (zpeer(d), f, h)))
    dir_l = net.copy(pp.at[right * 2 + 1], xr.at[2], xr.at[2], to_r)
    dir_r = net.copy(pp.at[left * 2], xr.at[3], xr.at[3], to_l)

    key = lax.broadcasted_iota(jnp.int32, (512, 256), 0)
    tok = lax.broadcasted_iota(jnp.int32, (512, 256), 1)
    inner = key - 256
    seen = ((key < 256) & (key < plen)) | ((key >= 256) & (inner <= tok) & (inner < rlen))
    bias[...] = jnp.where(seen, 0.0, -jnp.inf).astype(F32)
    live = lax.broadcasted_iota(jnp.int32, (256, 1024), 0) < rlen
    gm[...] = jnp.where(live, do_ref[...].astype(F32), 0.0).astype(BF16)
    kvb[0, 16:32] = sk_ref[...].reshape(16, 16, 128)
    kvb[1, 16:32] = sv_ref[...].reshape(16, 16, 128)
    acc[...] = jnp.zeros_like(acc)

    rel_l.wait_recv()
    xs[0] = xr[0] + pp[right * 2]
    com_l = net.copy(xs.at[0], xr.at[4], xr.at[4], to_r)
    rel_r.wait_recv()
    xs[1] = xr[1] + pp[left * 2 + 1]
    com_r = net.copy(xs.at[1], xr.at[5], xr.at[5], to_l)

    for m in ev_in:
        m.wait_recv()
    for k in range(NF):
        s = slots[k]
        sel[k, 0] = evk[s // 2, s % 2]
        sel[k, 1] = evv[s // 2, s % 2]
    kv_in = []
    for d in range(1, NF):
        src = (f + NF - d) % NF
        kv_in.append(net.copy(sel.at[fpeer(d)], kvb.at[:, f], kvb.at[:, src], (r, fpeer(d), h)))
    kvb[:, f] = sel[f]

    dir_r.wait_recv()
    com_l.wait_recv()
    half_a = pp[h * 2] + (xr[3] + xr[4])
    s1[0:4] = half_a.reshape(4, 16, 256)
    dir_l.wait_recv()
    com_r.wait_recv()
    half_b = pp[h * 2 + 1] + (xr[2] + xr[5])
    s1[4:8] = half_b.reshape(4, 16, 256)

    z_in = [
        net.copy(s1.at[zpeer(d)], zr.at[d], zr.at[d], (zpeer(d), f, h)) for d in range(1, NR)
    ]

    for m in kv_in:
        m.wait_recv()
    keys = kvb[0].reshape(512, 128)
    kt[...] = keys.astype(F32).T.astype(BF16)

    def head_step(k, carry):
        cols = pl.ds(pl.multiple_of(k * HD, HD), HD)
        q, g = q_ref[:, cols], gm[:, cols]
        s = mm(kvb[0].reshape(512, 128), q, 1, 1) * scale + bias[...]
        e = jnp.exp(s - jnp.max(s, axis=0, keepdims=True))
        p = (e * (1.0 / jnp.sum(e, axis=0, keepdims=True))).astype(BF16)
        dp = mm(kvb[1].reshape(512, 128), g, 1, 1)
        pw = p.astype(F32)
        ds = (pw * (dp - jnp.sum(pw * dp, axis=0, keepdims=True))).astype(BF16)
        dq_ref[:, cols] = (mm(kt[...], ds, 1, 0) * scale).T.astype(BF16)
        acc[0] += mm(ds, q, 1, 0)
        acc[1] += mm(p, g, 1, 0)
        return carry

    lax.fori_loop(0, 2, head_step, 0)

    for m in z_in:
        m.wait_recv()
    mine = s1[r]
    for d in range(1, NR):
        mine = mine + zr[d]
    spot = pl.ds(pl.multiple_of((r % 4) * 16, 16), 16)
    pf[h * 2 + r // 4, spot, :] = mine
    g_in = []
    for d in range(1, NR):
        src = (r + NR - d) % NR
        s_spot = pl.ds(pl.multiple_of((src % 4) * 16, 16), 16)
        here = pf.at[h * 2 + r // 4, spot]
        g_in.append(net.copy(here, here, pf.at[h * 2 + src // 4, s_spot], (zpeer(d), f, h)))

    lax.fori_loop(2, 4, head_step, 0)

    for m in g_in:
        m.wait_recv()
    def half(q, b):
        return pf.at[q * 2 + b]

    la = net.copy(half(h, 0), half(h, 0), half(left, 0), to_r)
    rb = net.copy(half(h, 1), half(h, 1), half(right, 1), to_l)
    lb = net.copy(half(h, 1), half(h, 1), half(left, 1), to_r)
    ra = net.copy(half(h, 0), half(h, 0), half(right, 0), to_l)

    lax.fori_loop(4, 5, head_step, 0)

    la.wait_recv()
    oa = net.copy(half(left, 0), half(left, 0), half(opp, 0), to_r)
    rb.wait_recv()
    ob = net.copy(half(right, 1), half(right, 1), half(opp, 1), to_l)

    lax.fori_loop(5, 6, head_step, 0)

    for m in (lb, ra, oa, ob):
        m.wait_recv()
    proj = pf[...].reshape(512, 256)
    gram = exact(proj, proj, 0, 0)
    cross = exact(total[...], proj, 0, 0)
    gy[0] = gram[0:192]
    gy[1, 0:64] = gram[192:256]
    gy[1, 64:192] = cross

    mate = (r, f + 1 - 2 * c, h)
    first = net.copy(gy.at[1 - c], fr, fr, mate)
    lax.fori_loop(6, 7, head_step, 0)
    first.wait_recv()
    gs[...] = (gy[c] + fr[...]).reshape(8, 24, 256)
    y_in = [
        net.copy(gs.at[ypeer(d)], yr.at[d], yr.at[d], (r, ypeer(d) * 2 + c, h))
        for d in range(1, 8)
    ]
    lax.fori_loop(7, 8, head_step, 0)

    k_all, v_all = acc[0] * scale, acc[1]
    kv_ref[0] = k_all[256:512].astype(BF16)
    kv_ref[1] = v_all[256:512].astype(BF16)
    ret[:, 0] = k_all[0:256].reshape(16, 16, 128)
    ret[:, 1] = v_all[0:256].reshape(16, 16, 128)

    for m in y_in:
        m.wait_recv()
    piece = gs[y]
    for d in range(1, 8):
        piece = piece + yr[d]
    gyf[c, y] = piece
    yg_in = []
    for d in range(1, 8):
        src = (y + 8 - d) % 8
        yg_in.append(
            net.copy(gyf.at[c, y], gyf.at[c, y], gyf.at[c, src], (r, ypeer(d) * 2 + c, h))
        )
    ret_arr = [
        net.copy(ret.at[fpeer(d)], ret_in.at[d], ret_in.at[d], (r, fpeer(d), h))
        for d in range(1, NF)
    ]
    for m in yg_in:
        m.wait_recv()
    last = net.copy(gyf.at[c], gyf.at[c], gyf.at[1 - c], mate)
    last.wait_recv()

    low = gyf[0].reshape(192, 256)
    high = gyf[1].reshape(192, 256)
    fa[...] = low[0:128, 0:128]
    g21 = jnp.concatenate([low[128:192, 0:128], high[0:64, 0:128]], 0)
    g22 = jnp.concatenate([low[128:192, 128:256], high[0:64, 128:256]], 0)
    whole_factor(fa, fx, li.at[0])
    i11 = li[0]
    l21 = exact(g21, i11, 1, 1)
    fa[...] = g22 - exact(l21, l21, 1, 1)
    li[2] = exact(l21, i11, 1, 0)

    for m in ret_arr:
        m.wait_recv()
    ret_in[0] = ret[f]
    for s in range(16):
        tot = jnp.zeros((2, 16, 128), F32)
        for d in range(NF):
            tot = tot + jnp.where(slot_at(slots, f, d) == s, ret_in[d], 0.0)
        bys[s // 2, :, s % 2] = tot
    b_in = [
        net.copy(bys.at[zpeer(d)], bys_in.at[d], bys_in.at[d], (zpeer(d), f, h))
        for d in range(1, NR)
    ]

    whole_factor(fa, fx, li.at[1])
    i22 = li[1]
    i21 = -exact(i22, li[2], 1, 0)

    def times_inverse(m):
        first_part = exact(m[:, 0:128], i11, 1, 1)
        second = exact(m[:, 0:128], i21, 1, 1) + exact(m[:, 128:256], i22, 1, 1)
        return first_part, second

    b1, b2 = times_inverse(gyf[1].reshape(192, 256)[64:192])
    back[:, 0:128] = b1
    back[:, 128:256] = b2
    bk = back[...]
    sq = jnp.sum(bk * bk, axis=0, keepdims=True)
    sqx[0] = sq
    x_in = [
        net.copy(sqx.at[0], sqx.at[d], sqx.at[d], (r, f, (h + d) % NH)) for d in range(1, NH)
    ]
    o1, o2 = times_inverse(pf[...].reshape(512, 256))
    orth[:, 0:128] = o1
    orth[:, 128:256] = o2
    for m in x_in:
        m.wait_recv()
    sqz[0] = (sqx[0] + sqx[2]) + (sqx[1] + sqx[3])
    q_in = [
        net.copy(sqz.at[0], sqz.at[d], sqz.at[d], (zpeer(d), f, h)) for d in range(1, NR)
    ]
    mo_ref[...] = total[...] - 0.05 * exact(orth[...], bk, 1, 1)
    for m in b_in:
        m.wait_recv()
    owned = bys[r]
    for d in range(1, NR):
        owned = owned + bys_in[d]
    pg_ref[...] = owned
    for m in q_in:
        m.wait_recv()
    squares = sqz[0]
    for d in range(1, NR):
        squares = squares + sqz[d]
    new = bk * lax.rsqrt(squares + 1e-06)
    bo_ref[...] = new
    upd_ref[...] = (GAIN * exact(orth[...], new, 1, 1)).astype(BF16)
    net.finish()


def slot_at(slots, f, d):
    at = (f + NF - d) % NF
    found = slots[0]
    for k in range(1, NF):
        found = jnp.where(at == k, slots[k], found)
    return found


def on_device(*args):
    vm = pl.BlockSpec(memory_space=pltpu.VMEM)
    sm = pl.BlockSpec(memory_space=pltpu.SMEM)
    v = pltpu.VMEM
    return pl.pallas_call(
        kernel,
        out_shape=(
            jax.ShapeDtypeStruct((256, 1024), BF16),
            jax.ShapeDtypeStruct((2, 256, 128), BF16),
            jax.ShapeDtypeStruct((2, 2, 16, 128), F32),
            jax.ShapeDtypeStruct((512, 128), BF16),
            jax.ShapeDtypeStruct((512, 128), F32),
            jax.ShapeDtypeStruct((128, 256), F32),
        ),
        in_specs=[vm] * 6 + [sm] * 4 + [vm] * 3,
        out_specs=(vm,) * 6,
        scratch_shapes=[
            v((512, 128), F32),
            v((8, 64, 256), F32),
            v((6, 64, 256), F32),
            v((2, 64, 256), F32),
            v((8, 16, 256), F32),
            v((8, 16, 256), F32),
            v((8, 64, 256), F32),
            v((2, 192, 256), F32),
            v((192, 256), F32),
            v((8, 24, 256), F32),
            v((8, 24, 256), F32),
            v((2, 8, 24, 256), F32),
            v((8, 2, 16, 128), BF16),
            v((8, 2, 16, 128), BF16),
            v((16, 2, 16, 128), BF16),
            v((2, 32, 16, 128), BF16),
            v((512, 256), F32),
            v((256, 1024), BF16),
            v((128, 512), BF16),
            v((2, 512, 128), F32),
            v((16, 2, 16, 128), F32),
            v((16, 2, 16, 128), F32),
            v((8, 2, 2, 16, 128), F32),
            v((8, 2, 2, 16, 128), F32),
            v((4, 1, 256), F32),
            v((8, 1, 256), F32),
            v((128, 128), F32),
            v((128, 128), F32),
            v((3, 128, 128), F32),
            v((512, 256), F32),
            v((128, 256), F32),
            pltpu.SemaphoreType.DMA((COPIES,)),
            pltpu.SemaphoreType.DMA((COPIES,)),
        ],
        compiler_params=pltpu.CompilerParams(collective_id=0, has_side_effects=True),
    )(*args)


def solution(mesh):
    placed = (
        P(("resp", "fsdp"), "head"),
        P(("resp", "fsdp"), "head"),
        P(("resp", "fsdp"), "head"),
        P(("resp", "fsdp"), "head"),
        P("resp", "fsdp", "head"),
        P("resp", "fsdp", "head"),
        P(),
        P(),
        P(),
        P(("resp", "fsdp")),
        P("fsdp", ("resp", "head")),
        P("fsdp", ("resp", "head")),
        P(("resp", "head"), None),
    )
    return jax.shard_map(
        on_device,
        mesh=mesh,
        in_specs=placed,
        out_specs=(
            P(("resp", "fsdp"), "head"),
            P(None, ("resp", "fsdp"), "head"),
            P(None, "resp", "fsdp", "head"),
            P("fsdp", ("resp", "head")),
            P("fsdp", ("resp", "head")),
            P(("resp", "head"), None),
        ),
        check_vma=False,
    )
```

time: 1100 us -> 113 us (0.10)
  the two profiles are of different devices: /device:TPU:32 before, /device:TPU:1 now
where the time goes in v1:
time: 113 us; the launch traced here: 112 us
  Pallas kernels  106 us (94%)
  local copies, waits for them, and re-layouts  5.51 us (5%)
  between operations  1.32 us (1%)
    pallas_call x1, Pallas kernels, on_device(): pl.pallas_call(kernel, out_shape=(jax.ShapeDtypeStruct((256, 1024), BF16)...  106 us
    unnamed x16, local copies, waits for them, and re-layouts  5.51 us

profile of v1, /device:TPU:1, one launch (start us, length us, event | category | flops | bytes accessed | tf_op | source)
XLA Modules:
  0.0 112.4 jit_solution(3640987908646593350)
XLA Ops:
  1.3 105.6 %shard_map.172 = (bf16[256,1024]{1,0:T(8,128)(2,1)}, bf16[2,256,128]{2,1,0:T(8,128)(2,1)}, f32[2,2,16,128]{3,2,1,0:T(8,128)}, bf16[512,128]{1,0:T(8,128)(2,1)}, f32[512,128]{1,0:T(8,128)}, /*index=5*/f32[128,256]{1,0:T(8,128)}) custom-call(bf16[256,1024]{1,0:T(8,128)(2,1)} %q_ref.1, bf16[256,128]{1,0:T(8,128)(2,1)} %sk_ref.1, bf16[256,128]{1,0:T(8,128)(2,1)} %sv_ref.1, ...), custom_call_target="tpu_custom_call" | custom-call | tf_op jit(solution)/shard_map/pallas_call | solution.py:401
  106.9 0.0 copy-start.3
  106.9 0.0 copy-start.4
  106.9 0.0 copy-start.2
  106.9 1.9 %copy.26 = bf16[256,1024]{1,0:T(8,128)(2,1)} copy(bf16[256,1024]{1,0:T(8,128)(2,1)} %get-tuple-element.12) | data formatting | bytes 1048576
  108.8 0.0 copy-done.3
  108.8 0.0 copy-start
  108.8 0.7 copy.27
  109.5 0.0 copy-done.4
  109.5 0.6 copy.28
  110.1 0.0 copy-done.2
  110.1 0.7 copy.29
  110.8 0.0 copy-done
  110.8 0.0 copy-start.1
  110.8 0.7 copy.30
  111.5 0.3 copy-done.1
  111.8 0.7 copy.31
Async XLA Ops:
  106.9 1.9 %copy-start.3 = (bf16[2,256,128]{2,1,0:T(8,128)(2,1)S(1)}, bf16[2,256,128]{2,1,0:T(8,128)(2,1)}, u32[]{:S(2)}) copy-start(bf16[2,256,128]{2,1,0:T(8,128)(2,1)} %get-tuple-element.13) | copy-start | bytes 393220
  106.9 2.6 %copy-start.4 = (f32[2,2,16,128]{3,2,1,0:T(8,128)S(1)}, f32[2,2,16,128]{3,2,1,0:T(8,128)}, u32[]{:S(2)}) copy-start(f32[2,2,16,128]{3,2,1,0:T(8,128)} %get-tuple-element.14) | copy-start | bytes 98308
  106.9 3.2 %copy-start.2 = (bf16[512,128]{1,0:T(8,128)(2,1)S(1)}, bf16[512,128]{1,0:T(8,128)(2,1)}, u32[]{:S(2)}) copy-start(bf16[512,128]{1,0:T(8,128)(2,1)} %get-tuple-element.15) | copy-start | bytes 393220
  108.8 1.9 %copy-start = (f32[512,128]{1,0:T(8,128)S(1)}, f32[512,128]{1,0:T(8,128)}, u32[]{:S(2)}) copy-start(f32[512,128]{1,0:T(8,128)} %get-tuple-element.16) | copy-start | bytes 786436
  110.8 1.0 copy-start.1

commit v2 on v1

--- a/solution.py
+++ b/solution.py
@@ -16,7 +16,7 @@
 HD = 128
 RANK = 256
 GAIN = math.sqrt(8192 * 4096 / 256)
-COPIES = 103
+COPIES = 126
 
 
 def mm(a, b, ca, cb, precision=None):
@@ -63,54 +63,81 @@
     def line(v, j):
         return jnp.broadcast_to(v[j : j + 1, :], (8, 128))
 
-    def lane(v, j):
-        return jnp.broadcast_to(v[:, j : j + 1], (8, 128))
-
-    def panel(p, carry):
-        at = pl.ds(pl.multiple_of(p * 8, 8), 8)
-        turn = lax.rem(128 - p * 8, 128)
-        z, zx = a_ref[at, :], x_ref[at, :]
-        turned = pltpu.roll(z, turn, 1)
-        cols = [lane(turned, j) for j in range(8)]
+    def lanes(v, start):
+        return [
+            jnp.take_along_axis(v, jnp.full((8, 128), start + j, jnp.int32), axis=1)
+            for j in range(8)
+        ]
+
+    def reciprocal(v):
+        guess = pl.reciprocal(v, approx=True)
+        guess = guess * (2.0 - v * guess)
+        return guess * (2.0 - v * guess)
+
+    def root(v):
+        guess = lax.rsqrt(v)
+        return guess * (1.5 - 0.5 * v * guess * guess)
+
+    def reduce_panel(z, zx, start):
+        cols = lanes(z, start)
         out = jnp.zeros((8, 128), F32)
-        for j in range(8):
-            pivot = line(cols[j], j)
-            inv = 1.0 / pivot
-            root = lax.rsqrt(pivot)
-            root = root * (1.5 - 0.5 * pivot * root * root)
-            coef = cols[j] * inv
-            here = row == j
-            zj, zxj = line(z, j), line(zx, j)
-            out = jnp.where(here, zxj * root, out)
-            z = jnp.where(here, zj * inv, z - coef * zj)
-            zx = jnp.where(here, zxj * inv, zx - coef * zxj)
-            for m in range(j + 1, 8):
-                cm = line(cols[m], j)
-                cols[m] = jnp.where(here, cm * inv, cols[m] - coef * cm)
+        for j in range(0, 8, 2):
+            one, two = row == j, row == j + 1
+            pair = one | two
+            a, b, d = line(cols[j], j), line(cols[j + 1], j), line(cols[j + 1], j + 1)
+            det = a * d - b * b
+            inv = reciprocal(det)
+            i11, i12, i22 = d * inv, -(b * inv), a * inv
+            f1 = jnp.where(one, -i11, jnp.where(two, -i12, cols[j] * i11 + cols[j + 1] * i12))
+            f2 = jnp.where(one, -i12, jnp.where(two, -i22, cols[j] * i12 + cols[j + 1] * i22))
+
+            def sweep(v):
+                return jnp.where(pair, 0.0, v) - (f1 * line(v, j) + f2 * line(v, j + 1))
+
+            first, second = line(zx, j), line(zx, j + 1)
+            up = reciprocal(a)
+            out = jnp.where(one, first * root(a), out)
+            out = jnp.where(two, (second - (b * up) * first) * root(det * up), out)
+            for m in range(j + 2, 8):
+                cols[m] = sweep(cols[m])
+            z, zx = sweep(z), sweep(zx)
+        return z, zx, out
+
+    def take(v, c, lines):
+        t = [c[j] * lines[j] for j in range(8)]
+        return v - (((t[0] + t[1]) + (t[2] + t[3])) + ((t[4] + t[5]) + (t[6] + t[7])))
+
+    z, zx, out = reduce_panel(a_ref[0:8, :], x_ref[0:8, :], 0)
+    o_ref[0:8, :] = out
+
+    def step(p, carry):
+        z, zx = carry
+        zs, zxs = [line(z, j) for j in range(8)], [line(zx, j) for j in range(8)]
+        at = pl.ds(pl.multiple_of(p * 8 + 8, 8), 8)
+        nz = a_ref[at, :]
+        c = lanes(nz, p * 8)
+        nz, nzx = take(nz, c, zs), take(x_ref[at, :], c, zxs)
+        nz, nzx, out = reduce_panel(nz, nzx, p * 8 + 8)
+        for t in range(2, 16):
+            below = jnp.where(p + 1 < t, 1.0, 0.0).astype(F32)
+            here = slice(8 * t, 8 * t + 8)
+            a_t = a_ref[here, :]
+            c = lanes(a_t * below, p * 8)
+            a_ref[here, :] = take(a_t, c, zs)
+            x_ref[here, :] = take(x_ref[here, :], c, zxs)
         o_ref[at, :] = out
-        zs = [line(z, j) for j in range(8)]
-        zxs = [line(zx, j) for j in range(8)]
-        for t in range(1, 16):
-            below = jnp.where(p < t, 1.0, 0.0).astype(F32)
-            a_t, x_t = a_ref[8 * t : 8 * t + 8, :], x_ref[8 * t : 8 * t + 8, :]
-            turned = pltpu.roll(a_t, turn, 1) * below
-            for j in range(8):
-                c = lane(turned, j)
-                a_t = a_t - c * zs[j]
-                x_t = x_t - c * zxs[j]
-            a_ref[8 * t : 8 * t + 8, :] = a_t
-            x_ref[8 * t : 8 * t + 8, :] = x_t
-        return carry
-
-    lax.fori_loop(0, 16, panel, 0)
+        return nz, nzx
+
+    lax.fori_loop(0, 15, step, (z, zx))
 
 
 def kernel(
-    q_ref, sk_ref, sv_ref, do_ref, pk_ref, pv_ref, counts_ref, owner_ref, pblk_ref, rblk_ref,
-    gq_ref, mom_ref, basis_ref,
+    q_hbm, sk_hbm, sv_hbm, do_hbm, pk_hbm, pv_hbm, counts_hbm, owner_hbm, pblk_hbm, rblk_ref,
+    gq_hbm, mom_hbm, basis_hbm,
     dq_ref, kv_ref, pg_ref, upd_ref, mo_ref, bo_ref,
-    total, pp, xr, xs, s1, zr, pf, gy, fr, gs, yr, gyf, evk, evv, sel, kvb, bias, gm, kt, acc,
-    ret, ret_in, bys, bys_in, sqx, sqz, fa, fx, li, orth, back, sent, arrived,
+    q_ref, sk_ref, sv_ref, do_ref, pk_ref, pv_ref, counts_ref, owner_ref, pblk_ref,
+    gq_ref, mom_ref, basis_ref, total, pp, xr, xs, s1, zr, pf, gy, fr, gs, yr, gyf, cy, cfr, cgs, cyr, cyf, evk, evv, sel, kvb, bias, gm, kt, acc,
+    ret, ret_in, bys, bys_in, sqx, sqz, fa, fx, li, orth, back, loaded, sent, arrived,
 ):
     r, f, h = lax.axis_index("resp"), lax.axis_index("fsdp"), lax.axis_index("head")
     y, c = f // 2, f % 2
@@ -135,9 +162,30 @@
     for d in range(1, NF):
         pl.semaphore_signal(barrier, inc=1, device_id=(r, fpeer(d), h), device_id_type=MESH)
 
+    def load(k, src, dst):
+        c = pltpu.make_async_copy(src, dst, loaded.at[k])
+        c.start()
+        return c
+
+    mains = [
+        load(0, mom_hbm, mom_ref), load(1, gq_hbm, gq_ref), load(2, basis_hbm, basis_ref),
+    ]
+    prompts = [
+        load(3, pk_hbm, pk_ref), load(4, pv_hbm, pv_ref), load(5, counts_hbm, counts_ref),
+        load(6, owner_hbm, owner_ref), load(7, pblk_hbm, pblk_ref),
+    ]
+    others = [
+        load(8, do_hbm, do_ref), load(9, sk_hbm, sk_ref), load(10, sv_hbm, sv_ref),
+        load(11, q_hbm, q_ref),
+    ]
+
+    for m in mains:
+        m.wait()
     total[...] = mom_ref[...] + gq_ref[...].astype(F32)
     for k in range(8):
         pp[k] = exact(total[64 * k : 64 * k + 64, :], basis_ref[...], 1, 0)
+    for m in prompts:
+        m.wait()
     evk[r] = pk_ref[...]
     evv[r] = pv_ref[...]
 
@@ -171,6 +219,8 @@
     dir_l = net.copy(pp.at[right * 2 + 1], xr.at[2], xr.at[2], to_r)
     dir_r = net.copy(pp.at[left * 2], xr.at[3], xr.at[3], to_l)
 
+    for m in others:
+        m.wait()
     key = lax.broadcasted_iota(jnp.int32, (512, 256), 0)
     tok = lax.broadcasted_iota(jnp.int32, (512, 256), 1)
     inner = key - 256
@@ -273,28 +323,22 @@
     for m in (lb, ra, oa, ob):
         m.wait_recv()
     proj = pf[...].reshape(512, 256)
-    gram = exact(proj, proj, 0, 0)
-    cross = exact(total[...], proj, 0, 0)
-    gy[0] = gram[0:192]
-    gy[1, 0:64] = gram[192:256]
-    gy[1, 64:192] = cross
+    p1, p2 = proj[:, 0:128], proj[:, 128:256]
+    g11, g21, g22 = exact(p1, p1, 0, 0), exact(p2, p1, 0, 0), exact(p2, p2, 0, 0)
+    gy[0, 0:128], gy[0, 128:192] = g11, g21[0:64]
+    gy[1, 0:64], gy[1, 64:192] = g21[64:128], g22
 
     mate = (r, f + 1 - 2 * c, h)
     first = net.copy(gy.at[1 - c], fr, fr, mate)
-    lax.fori_loop(6, 7, head_step, 0)
+    cross = exact(total[...], proj, 0, 0)
+    cy[0], cy[1] = cross[0:64], cross[64:128]
     first.wait_recv()
-    gs[...] = (gy[c] + fr[...]).reshape(8, 24, 256)
+    gs[...] = (gy[c] + fr[...]).reshape(8, 24, 128)
     y_in = [
         net.copy(gs.at[ypeer(d)], yr.at[d], yr.at[d], (r, ypeer(d) * 2 + c, h))
         for d in range(1, 8)
     ]
-    lax.fori_loop(7, 8, head_step, 0)
-
-    k_all, v_all = acc[0] * scale, acc[1]
-    kv_ref[0] = k_all[256:512].astype(BF16)
-    kv_ref[1] = v_all[256:512].astype(BF16)
-    ret[:, 0] = k_all[0:256].reshape(16, 16, 128)
-    ret[:, 1] = v_all[0:256].reshape(16, 16, 128)
+    lax.fori_loop(6, 8, head_step, 0)
 
     for m in y_in:
         m.wait_recv()
@@ -308,25 +352,52 @@
         yg_in.append(
             net.copy(gyf.at[c, y], gyf.at[c, y], gyf.at[c, src], (r, ypeer(d) * 2 + c, h))
         )
+    c_first = net.copy(cy.at[1 - c], cfr, cfr, mate)
+
+    k_all, v_all = acc[0] * scale, acc[1]
+    kv_ref[0] = k_all[256:512].astype(BF16)
+    kv_ref[1] = v_all[256:512].astype(BF16)
+    ret[:, 0] = k_all[0:256].reshape(16, 16, 128).astype(BF16)
+    ret[:, 1] = v_all[0:256].reshape(16, 16, 128).astype(BF16)
+
+    for m in yg_in:
+        m.wait_recv()
+    last = net.copy(gyf.at[c], gyf.at[c], gyf.at[1 - c], mate)
+    c_first.wait_recv()
+    cgs[...] = (cy[c] + cfr[...]).reshape(8, 8, 256)
+    c_in = [
+        net.copy(cgs.at[ypeer(d)], cyr.at[d], cyr.at[d], (r, ypeer(d) * 2 + c, h))
+        for d in range(1, 8)
+    ]
     ret_arr = [
         net.copy(ret.at[fpeer(d)], ret_in.at[d], ret_in.at[d], (r, fpeer(d), h))
         for d in range(1, NF)
     ]
-    for m in yg_in:
-        m.wait_recv()
-    last = net.copy(gyf.at[c], gyf.at[c], gyf.at[1 - c], mate)
     last.wait_recv()
 
-    low = gyf[0].reshape(192, 256)
-    high = gyf[1].reshape(192, 256)
-    fa[...] = low[0:128, 0:128]
-    g21 = jnp.concatenate([low[128:192, 0:128], high[0:64, 0:128]], 0)
-    g22 = jnp.concatenate([low[128:192, 128:256], high[0:64, 128:256]], 0)
+    low = gyf[0].reshape(192, 128)
+    high = gyf[1].reshape(192, 128)
+    fa[...] = low[0:128]
+    li[1, 0:64], li[1, 64:128] = low[128:192], high[0:64]
+    li[3] = high[64:192]
     whole_factor(fa, fx, li.at[0])
     i11 = li[0]
-    l21 = exact(g21, i11, 1, 1)
-    fa[...] = g22 - exact(l21, l21, 1, 1)
+    l21 = exact(li[1], i11, 1, 1)
+    fa[...] = li[3] - exact(l21, l21, 1, 1)
     li[2] = exact(l21, i11, 1, 0)
+
+    for m in c_in:
+        m.wait_recv()
+    c_piece = cgs[y]
+    for d in range(1, 8):
+        c_piece = c_piece + cyr[d]
+    cyf[c, y] = c_piece
+    cg_in = []
+    for d in range(1, NF):
+        src = (f + NF - d) % NF
+        cg_in.append(
+            net.copy(cyf.at[c, y], cyf.at[c, y], cyf.at[src % 2, src // 2], (r, fpeer(d), h))
+        )
 
     for m in ret_arr:
         m.wait_recv()
@@ -334,7 +405,7 @@
     for s in range(16):
         tot = jnp.zeros((2, 16, 128), F32)
         for d in range(NF):
-            tot = tot + jnp.where(slot_at(slots, f, d) == s, ret_in[d], 0.0)
+            tot = tot + jnp.where(slot_at(slots, f, d) == s, ret_in[d].astype(F32), 0.0)
         bys[s // 2, :, s % 2] = tot
     b_in = [
         net.copy(bys.at[zpeer(d)], bys_in.at[d], bys_in.at[d], (zpeer(d), f, h))
@@ -350,7 +421,9 @@
         second = exact(m[:, 0:128], i21, 1, 1) + exact(m[:, 128:256], i22, 1, 1)
         return first_part, second
 
-    b1, b2 = times_inverse(gyf[1].reshape(192, 256)[64:192])
+    for m in cg_in:
+        m.wait_recv()
+    b1, b2 = times_inverse(cyf[...].reshape(128, 256))
     back[:, 0:128] = b1
     back[:, 128:256] = b2
     bk = back[...]
@@ -394,23 +467,37 @@
     return found
 
 
+def put(*refs):
+    moves = [pltpu.make_async_copy(refs[k], refs[6 + k], refs[12].at[k]) for k in range(6)]
+    for m in moves:
+        m.start()
+    for m in moves:
+        m.wait()
+
+
 def on_device(*args):
     vm = pl.BlockSpec(memory_space=pltpu.VMEM)
-    sm = pl.BlockSpec(memory_space=pltpu.SMEM)
+    hb = pl.BlockSpec(memory_space=pltpu.HBM)
     v = pltpu.VMEM
-    return pl.pallas_call(
-        kernel,
-        out_shape=(
+    outs = (
             jax.ShapeDtypeStruct((256, 1024), BF16),
             jax.ShapeDtypeStruct((2, 256, 128), BF16),
             jax.ShapeDtypeStruct((2, 2, 16, 128), F32),
             jax.ShapeDtypeStruct((512, 128), BF16),
             jax.ShapeDtypeStruct((512, 128), F32),
             jax.ShapeDtypeStruct((128, 256), F32),
-        ),
-        in_specs=[vm] * 6 + [sm] * 4 + [vm] * 3,
+    )
+    s = pltpu.SMEM
+    done = pl.pallas_call(
+        kernel,
+        out_shape=outs,
+        in_specs=[hb] * 9 + [pl.BlockSpec(memory_space=pltpu.SMEM)] + [hb] * 3,
         out_specs=(vm,) * 6,
         scratch_shapes=[
+            v((256, 1024), BF16), v((256, 128), BF16), v((256, 128), BF16), v((256, 1024), BF16),
+            v((2, 16, 128), BF16), v((2, 16, 128), BF16), s((16,), jnp.int32),
+            s((16,), jnp.int32), s((16,), jnp.int32), v((512, 128), BF16), v((512, 128), F32),
+            v((128, 256), F32),
             v((512, 128), F32),
             v((8, 64, 256), F32),
             v((6, 64, 256), F32),
@@ -418,11 +505,16 @@
             v((8, 16, 256), F32),
             v((8, 16, 256), F32),
             v((8, 64, 256), F32),
-            v((2, 192, 256), F32),
-            v((192, 256), F32),
-            v((8, 24, 256), F32),
-            v((8, 24, 256), F32),
-            v((2, 8, 24, 256), F32),
+            v((2, 192, 128), F32),
+            v((192, 128), F32),
+            v((8, 24, 128), F32),
+            v((8, 24, 128), F32),
+            v((2, 8, 24, 128), F32),
+            v((2, 64, 256), F32),
+            v((64, 256), F32),
+            v((8, 8, 256), F32),
+            v((8, 8, 256), F32),
+            v((2, 8, 8, 256), F32),
             v((8, 2, 16, 128), BF16),
             v((8, 2, 16, 128), BF16),
             v((16, 2, 16, 128), BF16),
@@ -431,22 +523,33 @@
             v((256, 1024), BF16),
             v((128, 512), BF16),
             v((2, 512, 128), F32),
-            v((16, 2, 16, 128), F32),
-            v((16, 2, 16, 128), F32),
+            v((16, 2, 16, 128), BF16),
+            v((16, 2, 16, 128), BF16),
             v((8, 2, 2, 16, 128), F32),
             v((8, 2, 2, 16, 128), F32),
             v((4, 1, 256), F32),
             v((8, 1, 256), F32),
             v((128, 128), F32),
             v((128, 128), F32),
-            v((3, 128, 128), F32),
+            v((4, 128, 128), F32),
             v((512, 256), F32),
             v((128, 256), F32),
+            pltpu.SemaphoreType.DMA((12,)),
             pltpu.SemaphoreType.DMA((COPIES,)),
             pltpu.SemaphoreType.DMA((COPIES,)),
         ],
-        compiler_params=pltpu.CompilerParams(collective_id=0, has_side_effects=True),
-    )(*args)
+        compiler_params=pltpu.CompilerParams(
+            collective_id=0, has_side_effects=True, vmem_limit_bytes=24 * 1024 * 1024
+        ),
+    )(*[a if k == 9 else pltpu.with_memory_space_constraint(a, pltpu.HBM) for k, a in enumerate(args)])
+    return pl.pallas_call(
+        put,
+        out_shape=outs,
+        in_specs=[vm] * 6,
+        out_specs=(hb,) * 6,
+        scratch_shapes=[pltpu.SemaphoreType.DMA((6,))],
+        compiler_params=pltpu.CompilerParams(vmem_limit_bytes=24 * 1024 * 1024),
+    )(*done)
 
 
 def solution(mesh):

time: 113 us -> 86.1 us (0.76)
  Pallas kernels: 106 us -> 84.7 us
  local copies, waits for them, and re-layouts: 5.51 us -> 0 us
    pallas_call x1 -> x2, Pallas kernels: 106 us -> 84.7 us  [the longest x1 83.6 us: on_device(): pl.pallas_call(kernel, out_shape=outs, in_specs=[hb] * 9 + [pl.BlockSpec(...]
    unnamed x16 -> x0, local copies, waits for them, and re-layouts: 5.51 us -> none
where the time goes in v2:
time: 86.1 us; the launch traced here: 86 us
  Pallas kernels  84.7 us (98%)
  between operations  1.29 us (1%)
    pallas_call x1, Pallas kernels, on_device(): pl.pallas_call(kernel, out_shape=outs, in_specs=[hb] * 9 + [pl.BlockSpec(...  83.6 us

profile of v2, /device:TPU:1, one launch (start us, length us, event | category | flops | bytes accessed | tf_op | source)
XLA Modules:
  0.0 86.0 jit_solution(1181007998087298006)
XLA Ops:
  1.3 83.6 %shard_map.172 = (bf16[256,1024]{1,0:T(8,128)(2,1)S(1)}, bf16[2,256,128]{2,1,0:T(8,128)(2,1)S(1)}, f32[2,2,16,128]{3,2,1,0:T(8,128)S(1)}, bf16[512,128]{1,0:T(8,...) custom-call(bf16[256,1024]{1,0:T(8,128)(2,1)} %q_hbm.1, bf16[256,128]{1,0:T(8,128)(2,1)} %sk_hbm.1, ...), custom_call_target="tpu_custom_call" | custom-call | tf_op jit(solution)/shard_map/pallas_call | solution.py:491
  84.9 1.1 %shard_map.173 = (bf16[256,1024]{1,0:T(8,128)(2,1)}, bf16[2,256,128]{2,1,0:T(8,128)(2,1)}, f32[2,2,16,128]{3,2,1,0:T(8,128)}, bf16[512,128]{1,0:T(8,128)(2,1)}, f32[512,128]{1,0:T(8,128)}, /*index=5*/f32[128,256]{1,0:T(8,128)}) custom-call(bf16[256,1024]{1,0:T(8,128)(2,1)S(1)} %get-tuple-element.12.refs_0_, ...), custom_call_target="tpu_custom_call" | custom-call | tf_op jit(solution)/shard_map/pallas_call | solution.py:545

commit v3 on v2

--- a/solution.py
+++ b/solution.py
@@ -1,3 +1,4 @@
+import functools
 import math
 
 import jax
@@ -16,7 +17,7 @@
 HD = 128
 RANK = 256
 GAIN = math.sqrt(8192 * 4096 / 256)
-COPIES = 126
+COPIES = 176
 
 
 def mm(a, b, ca, cb, precision=None):
@@ -80,14 +81,20 @@
 
     def reduce_panel(z, zx, start):
         cols = lanes(z, start)
+        spread = {(i, k): line(cols[k], i) for k in range(8) for i in range(k, 8)}
         out = jnp.zeros((8, 128), F32)
         for j in range(0, 8, 2):
             one, two = row == j, row == j + 1
             pair = one | two
-            a, b, d = line(cols[j], j), line(cols[j + 1], j), line(cols[j + 1], j + 1)
+            a, b, d = spread[j, j], spread[j + 1, j], spread[j + 1, j + 1]
             det = a * d - b * b
             inv = reciprocal(det)
             i11, i12, i22 = d * inv, -(b * inv), a * inv
+            for i in range(j + 2, 8):
+                e1 = spread[i, j] * i11 + spread[i, j + 1] * i12
+                e2 = spread[i, j] * i12 + spread[i, j + 1] * i22
+                for k in range(j + 2, i + 1):
+                    spread[i, k] = spread[i, k] - (e1 * spread[k, j] + e2 * spread[k, j + 1])
             f1 = jnp.where(one, -i11, jnp.where(two, -i12, cols[j] * i11 + cols[j + 1] * i12))
             f2 = jnp.where(one, -i12, jnp.where(two, -i22, cols[j] * i12 + cols[j + 1] * i22))
 
@@ -110,7 +117,7 @@
     z, zx, out = reduce_panel(a_ref[0:8, :], x_ref[0:8, :], 0)
     o_ref[0:8, :] = out
 
-    def step(p, carry):
+    def step(first, p, carry):
         z, zx = carry
         zs, zxs = [line(z, j) for j in range(8)], [line(zx, j) for j in range(8)]
         at = pl.ds(pl.multiple_of(p * 8 + 8, 8), 8)
@@ -118,7 +125,7 @@
         c = lanes(nz, p * 8)
         nz, nzx = take(nz, c, zs), take(x_ref[at, :], c, zxs)
         nz, nzx, out = reduce_panel(nz, nzx, p * 8 + 8)
-        for t in range(2, 16):
+        for t in range(first, 16):
             below = jnp.where(p + 1 < t, 1.0, 0.0).astype(F32)
             here = slice(8 * t, 8 * t + 8)
             a_t = a_ref[here, :]
@@ -128,16 +135,18 @@
         o_ref[at, :] = out
         return nz, nzx
 
-    lax.fori_loop(0, 15, step, (z, zx))
+    carry = (z, zx)
+    for low, high in ((0, 4), (4, 8), (8, 12), (12, 15)):
+        carry = lax.fori_loop(low, high, functools.partial(step, low + 2), carry)
 
 
 def kernel(
     q_hbm, sk_hbm, sv_hbm, do_hbm, pk_hbm, pv_hbm, counts_hbm, owner_hbm, pblk_hbm, rblk_ref,
     gq_hbm, mom_hbm, basis_hbm,
     dq_ref, kv_ref, pg_ref, upd_ref, mo_ref, bo_ref,
-    q_ref, sk_ref, sv_ref, do_ref, pk_ref, pv_ref, counts_ref, owner_ref, pblk_ref,
-    gq_ref, mom_ref, basis_ref, total, pp, xr, xs, s1, zr, pf, gy, fr, gs, yr, gyf, cy, cfr, cgs, cyr, cyf, evk, evv, sel, kvb, bias, gm, kt, acc,
-    ret, ret_in, bys, bys_in, sqx, sqz, fa, fx, li, orth, back, loaded, sent, arrived,
+    q_ref, sk_ref, sv_ref, do_ref, pkv_ref, counts_ref, owner_ref, pblk_ref,
+    gq_ref, mom_ref, basis_ref, total, pp, xr, xs, s1, zr, pf, gy, fr, gs, yr, gyf, cy, cfr, cgs, cyr, cyf, ev, sel, kvb, bias, gm, kt, acc,
+    ret, ret_in, bys, bys_in, sqz, fa, fx, li, orth, back, loaded, sent, arrived,
 ):
     r, f, h = lax.axis_index("resp"), lax.axis_index("fsdp"), lax.axis_index("head")
     y, c = f // 2, f % 2
@@ -154,14 +163,6 @@
     def ypeer(d):
         return (y + d) % 8
 
-    barrier = pltpu.get_barrier_semaphore()
-    for d in range(1, NH):
-        pl.semaphore_signal(barrier, inc=1, device_id=(r, f, (h + d) % NH), device_id_type=MESH)
-    for d in range(1, NR):
-        pl.semaphore_signal(barrier, inc=1, device_id=(zpeer(d), f, h), device_id_type=MESH)
-    for d in range(1, NF):
-        pl.semaphore_signal(barrier, inc=1, device_id=(r, fpeer(d), h), device_id_type=MESH)
-
     def load(k, src, dst):
         c = pltpu.make_async_copy(src, dst, loaded.at[k])
         c.start()
@@ -171,7 +172,7 @@
         load(0, mom_hbm, mom_ref), load(1, gq_hbm, gq_ref), load(2, basis_hbm, basis_ref),
     ]
     prompts = [
-        load(3, pk_hbm, pk_ref), load(4, pv_hbm, pv_ref), load(5, counts_hbm, counts_ref),
+        load(3, pk_hbm, pkv_ref.at[0]), load(4, pv_hbm, pkv_ref.at[1]), load(5, counts_hbm, counts_ref),
         load(6, owner_hbm, owner_ref), load(7, pblk_hbm, pblk_ref),
     ]
     others = [
@@ -179,16 +180,65 @@
         load(11, q_hbm, q_ref),
     ]
 
+    barrier = pltpu.get_barrier_semaphore()
+    for d in range(1, NR * NH):
+        pl.semaphore_signal(
+            barrier, inc=1, device_id=(zpeer(d // NH), f, (h + d) % NH), device_id_type=MESH
+        )
+    for d in range(1, NF):
+        pl.semaphore_signal(barrier, inc=1, device_id=(r, fpeer(d), h), device_id_type=MESH)
+
+    opp = (h + 2) % NH
+    to_r, to_l = (r, f, right), (r, f, left)
+
     for m in mains:
         m.wait()
     total[...] = mom_ref[...] + gq_ref[...].astype(F32)
-    for k in range(8):
-        pp[k] = exact(total[64 * k : 64 * k + 64, :], basis_ref[...], 1, 0)
+
+    def project(q):
+        rows = total[pl.ds(pl.multiple_of(q * 128, 128), 128), :]
+        pp[pl.ds(q * 8, 8)] = exact(rows, basis_ref[...], 1, 0).reshape(8, 16, 256)
+
+    project(opp)
+    pl.semaphore_wait(barrier, (NR * NH - 1) + (NF - 1))
+
+    order = (2, 1, 3, 0)
+    slot = [((r // 2 + e) % 4) * 2 for e in range(4)]
+    rel_l, rel_r, dir_l, dir_r, com_l, com_r = {}, {}, {}, {}, {}, {}
+    for e in order:
+        rel_l[e] = net.copy(pp.at[opp * 8 + slot[e]], xr.at[0, e], xr.at[0, e], to_r)
+        rel_r[e] = net.copy(pp.at[opp * 8 + slot[e] + 1], xr.at[1, e], xr.at[1, e], to_l)
     for m in prompts:
         m.wait()
-    evk[r] = pk_ref[...]
-    evv[r] = pv_ref[...]
-
+    ev_in = []
+    for d in range(1, NR):
+        src = (r + NR - d) % NR
+        ev_in.append(net.copy(pkv_ref, ev.at[r], ev.at[src], (zpeer(d), f, h)))
+    project(right)
+    project(left)
+    for e in order:
+        dir_l[e] = net.copy(pp.at[right * 8 + slot[e] + 1], xr.at[2, e], xr.at[2, e], to_r)
+        dir_r[e] = net.copy(pp.at[left * 8 + slot[e]], xr.at[3, e], xr.at[3, e], to_l)
+        rel_l[e].wait_recv()
+        xs[0, e] = xr[0, e] + pp[right * 8 + slot[e]]
+        com_l[e] = net.copy(xs.at[0, e], xr.at[4, e], xr.at[4, e], to_r)
+        rel_r[e].wait_recv()
+        xs[1, e] = xr[1, e] + pp[left * 8 + slot[e] + 1]
+        com_r[e] = net.copy(xs.at[1, e], xr.at[5, e], xr.at[5, e], to_l)
+    project(h)
+
+    z_in = []
+    ready = {2: (4,), 1: (2,), 3: (3, 5, 6), 0: (1, 7)}
+    for e in order:
+        for m in (dir_l, dir_r, com_l, com_r):
+            m[e].wait_recv()
+        even, odd = slot[e], slot[e] + 1
+        s1[even] = pp[h * 8 + even] + (xr[3, e] + xr[4, e])
+        s1[odd] = pp[h * 8 + odd] + (xr[2, e] + xr[5, e])
+        for d in ready[e]:
+            z_in.append(net.copy(s1.at[zpeer(d)], zr.at[d], zr.at[d], (zpeer(d), f, h)))
+
+    ev[r] = pkv_ref[...]
     ends = []
     run = jnp.int32(0)
     for g in range(16):
@@ -204,20 +254,17 @@
     slots = [owner_ref[group_of(r * NF + k)] for k in range(NF)]
     plen = pblk_ref[group_of(r * NF + f)] * 128
     rlen = rblk_ref[0] * 128
-
-    pl.semaphore_wait(barrier, (NH - 1) + (NR - 1) + (NF - 1))
-
-    opp = (h + 2) % NH
-    to_r, to_l = (r, f, right), (r, f, left)
-    rel_l = net.copy(pp.at[opp * 2], xr.at[0], xr.at[0], to_r)
-    rel_r = net.copy(pp.at[opp * 2 + 1], xr.at[1], xr.at[1], to_l)
-    ev_in = []
-    for d in range(1, NR):
-        src = (r + NR - d) % NR
-        ev_in.append(net.copy(pk_ref, evk.at[r], evk.at[src], (zpeer(d), f, h)))
-        ev_in.append(net.copy(pv_ref, evv.at[r], evv.at[src], (zpeer(d), f, h)))
-    dir_l = net.copy(pp.at[right * 2 + 1], xr.at[2], xr.at[2], to_r)
-    dir_r = net.copy(pp.at[left * 2], xr.at[3], xr.at[3], to_l)
+    for m in ev_in:
+        m.wait_recv()
+    for k in range(NF):
+        sl = slots[k]
+        sel[k, 0] = ev[sl // 2, 0, sl % 2]
+        sel[k, 1] = ev[sl // 2, 1, sl % 2]
+    kv_in = []
+    for d in range(1, NF):
+        src = (f + NF - d) % NF
+        kv_in.append(net.copy(sel.at[fpeer(d)], kvb.at[:, f], kvb.at[:, src], (r, fpeer(d), h)))
+    kvb[:, f] = sel[f]
 
     for m in others:
         m.wait()
@@ -231,43 +278,6 @@
     kvb[0, 16:32] = sk_ref[...].reshape(16, 16, 128)
     kvb[1, 16:32] = sv_ref[...].reshape(16, 16, 128)
     acc[...] = jnp.zeros_like(acc)
-
-    rel_l.wait_recv()
-    xs[0] = xr[0] + pp[right * 2]
-    com_l = net.copy(xs.at[0], xr.at[4], xr.at[4], to_r)
-    rel_r.wait_recv()
-    xs[1] = xr[1] + pp[left * 2 + 1]
-    com_r = net.copy(xs.at[1], xr.at[5], xr.at[5], to_l)
-
-    for m in ev_in:
-        m.wait_recv()
-    for k in range(NF):
-        s = slots[k]
-        sel[k, 0] = evk[s // 2, s % 2]
-        sel[k, 1] = evv[s // 2, s % 2]
-    kv_in = []
-    for d in range(1, NF):
-        src = (f + NF - d) % NF
-        kv_in.append(net.copy(sel.at[fpeer(d)], kvb.at[:, f], kvb.at[:, src], (r, fpeer(d), h)))
-    kvb[:, f] = sel[f]
-
-    dir_r.wait_recv()
-    com_l.wait_recv()
-    half_a = pp[h * 2] + (xr[3] + xr[4])
-    s1[0:4] = half_a.reshape(4, 16, 256)
-    dir_l.wait_recv()
-    com_r.wait_recv()
-    half_b = pp[h * 2 + 1] + (xr[2] + xr[5])
-    s1[4:8] = half_b.reshape(4, 16, 256)
-
-    z_in = [
-        net.copy(s1.at[zpeer(d)], zr.at[d], zr.at[d], (zpeer(d), f, h)) for d in range(1, NR)
-    ]
-
-    for m in kv_in:
-        m.wait_recv()
-    keys = kvb[0].reshape(512, 128)
-    kt[...] = keys.astype(F32).T.astype(BF16)
 
     def head_step(k, carry):
         cols = pl.ds(pl.multiple_of(k * HD, HD), HD)
@@ -283,54 +293,82 @@
         acc[1] += mm(p, g, 1, 0)
         return carry
 
-    lax.fori_loop(0, 2, head_step, 0)
-
     for m in z_in:
         m.wait_recv()
     mine = s1[r]
     for d in range(1, NR):
         mine = mine + zr[d]
-    spot = pl.ds(pl.multiple_of((r % 4) * 16, 16), 16)
-    pf[h * 2 + r // 4, spot, :] = mine
-    g_in = []
+    pf[h * 8 + r] = mine
+    g_in = [None]
     for d in range(1, NR):
         src = (r + NR - d) % NR
-        s_spot = pl.ds(pl.multiple_of((src % 4) * 16, 16), 16)
-        here = pf.at[h * 2 + r // 4, spot]
-        g_in.append(net.copy(here, here, pf.at[h * 2 + src // 4, s_spot], (zpeer(d), f, h)))
-
-    lax.fori_loop(2, 4, head_step, 0)
-
-    for m in g_in:
-        m.wait_recv()
-    def half(q, b):
-        return pf.at[q * 2 + b]
-
-    la = net.copy(half(h, 0), half(h, 0), half(left, 0), to_r)
-    rb = net.copy(half(h, 1), half(h, 1), half(right, 1), to_l)
-    lb = net.copy(half(h, 1), half(h, 1), half(left, 1), to_r)
-    ra = net.copy(half(h, 0), half(h, 0), half(right, 0), to_l)
-
-    lax.fori_loop(4, 5, head_step, 0)
-
-    la.wait_recv()
-    oa = net.copy(half(left, 0), half(left, 0), half(opp, 0), to_r)
-    rb.wait_recv()
-    ob = net.copy(half(right, 1), half(right, 1), half(opp, 1), to_l)
-
-    lax.fori_loop(5, 6, head_step, 0)
-
-    for m in (lb, ra, oa, ob):
-        m.wait_recv()
-    proj = pf[...].reshape(512, 256)
-    p1, p2 = proj[:, 0:128], proj[:, 128:256]
-    g11, g21, g22 = exact(p1, p1, 0, 0), exact(p2, p1, 0, 0), exact(p2, p2, 0, 0)
+        here = pf.at[h * 8 + r]
+        g_in.append(net.copy(here, here, pf.at[h * 8 + src], (zpeer(d), f, h)))
+    from_l, from_r, passed = {}, {}, []
+
+    def spread(d):
+        at = (r + NR - d) % NR
+        here = pf.at[h * 8 + at]
+        from_l[d] = net.copy(here, here, pf.at[left * 8 + at], to_r)
+        from_r[d] = net.copy(here, here, pf.at[right * 8 + at], to_l)
+
+    def relay(d):
+        at = (r + NR - d) % NR
+        if d % 2 == 0:
+            from_l[d].wait_recv()
+            here, there = pf.at[left * 8 + at], to_r
+        else:
+            from_r[d].wait_recv()
+            here, there = pf.at[right * 8 + at], to_l
+        passed.append(net.copy(here, here, pf.at[opp * 8 + at], there))
+
+    spread(0)
+    for m in kv_in:
+        m.wait_recv()
+    keys = kvb[0].reshape(512, 128)
+    kt[...] = keys.astype(F32).T.astype(BF16)
+    g_in[1].wait_recv()
+    spread(1)
+    g_in[7].wait_recv()
+    spread(7)
+    relay(0)
+    lax.fori_loop(0, 1, head_step, 0)
+    for one, two in ((2, 6), (3, 5)):
+        g_in[one].wait_recv()
+        spread(one)
+        g_in[two].wait_recv()
+        spread(two)
+        if one == 2:
+            relay(1)
+            relay(7)
+    g_in[4].wait_recv()
+    spread(4)
+    relay(2)
+    relay(6)
+    lax.fori_loop(1, 2, head_step, 0)
+    relay(3)
+    relay(5)
+    relay(4)
+    for d in range(NR):
+        (from_r if d % 2 == 0 else from_l)[d].wait_recv()
+
+    def gram_of(m):
+        m1, m2 = m[:, 0:128], m[:, 128:256]
+        return exact(m1, m1, 0, 0), exact(m2, m1, 0, 0), exact(m2, m2, 0, 0)
+
+    def quarter(q):
+        return pf[pl.ds(q * 8, 8)].reshape(128, 256)
+
+    part = gram_of(jnp.concatenate([quarter(h), quarter(left), quarter(right)], 0))
+    for m in passed:
+        m.wait_recv()
+    g11, g21, g22 = (a + b for a, b in zip(part, gram_of(quarter(opp))))
     gy[0, 0:128], gy[0, 128:192] = g11, g21[0:64]
     gy[1, 0:64], gy[1, 64:192] = g21[64:128], g22
 
     mate = (r, f + 1 - 2 * c, h)
     first = net.copy(gy.at[1 - c], fr, fr, mate)
-    cross = exact(total[...], proj, 0, 0)
+    cross = exact(total[...], pf[...].reshape(512, 256), 0, 0)
     cy[0], cy[1] = cross[0:64], cross[64:128]
     first.wait_recv()
     gs[...] = (gy[c] + fr[...]).reshape(8, 24, 128)
@@ -338,7 +376,7 @@
         net.copy(gs.at[ypeer(d)], yr.at[d], yr.at[d], (r, ypeer(d) * 2 + c, h))
         for d in range(1, 8)
     ]
-    lax.fori_loop(6, 8, head_step, 0)
+    lax.fori_loop(2, 5, head_step, 0)
 
     for m in y_in:
         m.wait_recv()
@@ -354,6 +392,7 @@
         )
     c_first = net.copy(cy.at[1 - c], cfr, cfr, mate)
 
+    lax.fori_loop(5, 8, head_step, 0)
     k_all, v_all = acc[0] * scale, acc[1]
     kv_ref[0] = k_all[256:512].astype(BF16)
     kv_ref[1] = v_all[256:512].astype(BF16)
@@ -428,19 +467,14 @@
     back[:, 128:256] = b2
     bk = back[...]
     sq = jnp.sum(bk * bk, axis=0, keepdims=True)
-    sqx[0] = sq
-    x_in = [
-        net.copy(sqx.at[0], sqx.at[d], sqx.at[d], (r, f, (h + d) % NH)) for d in range(1, NH)
-    ]
+    sqz[0] = sq
+    q_in = []
+    for d in range(1, NR * NH):
+        peer = (zpeer(d // NH), f, (h + d) % NH)
+        q_in.append(net.copy(sqz.at[0], sqz.at[d], sqz.at[d], peer))
     o1, o2 = times_inverse(pf[...].reshape(512, 256))
     orth[:, 0:128] = o1
     orth[:, 128:256] = o2
-    for m in x_in:
-        m.wait_recv()
-    sqz[0] = (sqx[0] + sqx[2]) + (sqx[1] + sqx[3])
-    q_in = [
-        net.copy(sqz.at[0], sqz.at[d], sqz.at[d], (zpeer(d), f, h)) for d in range(1, NR)
-    ]
     mo_ref[...] = total[...] - 0.05 * exact(orth[...], bk, 1, 1)
     for m in b_in:
         m.wait_recv()
@@ -448,15 +482,16 @@
     for d in range(1, NR):
         owned = owned + bys_in[d]
     pg_ref[...] = owned
+    net.finish()
     for m in q_in:
         m.wait_recv()
     squares = sqz[0]
-    for d in range(1, NR):
+    for d in range(1, NR * NH):
         squares = squares + sqz[d]
     new = bk * lax.rsqrt(squares + 1e-06)
     bo_ref[...] = new
     upd_ref[...] = (GAIN * exact(orth[...], new, 1, 1)).astype(BF16)
-    net.finish()
+    assert net.n == COPIES
 
 
 def slot_at(slots, f, d):
@@ -495,16 +530,16 @@
         out_specs=(vm,) * 6,
         scratch_shapes=[
             v((256, 1024), BF16), v((256, 128), BF16), v((256, 128), BF16), v((256, 1024), BF16),
-            v((2, 16, 128), BF16), v((2, 16, 128), BF16), s((16,), jnp.int32),
+            v((2, 2, 16, 128), BF16), s((16,), jnp.int32),
             s((16,), jnp.int32), s((16,), jnp.int32), v((512, 128), BF16), v((512, 128), F32),
             v((128, 256), F32),
             v((512, 128), F32),
-            v((8, 64, 256), F32),
-            v((6, 64, 256), F32),
-            v((2, 64, 256), F32),
+            v((32, 16, 256), F32),
+            v((6, 4, 16, 256), F32),
+            v((2, 4, 16, 256), F32),
             v((8, 16, 256), F32),
             v((8, 16, 256), F32),
-            v((8, 64, 256), F32),
+            v((32, 16, 256), F32),
             v((2, 192, 128), F32),
             v((192, 128), F32),
             v((8, 24, 128), F32),
@@ -515,8 +550,7 @@
             v((8, 8, 256), F32),
             v((8, 8, 256), F32),
             v((2, 8, 8, 256), F32),
-            v((8, 2, 16, 128), BF16),
-            v((8, 2, 16, 128), BF16),
+            v((8, 2, 2, 16, 128), BF16),
             v((16, 2, 16, 128), BF16),
             v((2, 32, 16, 128), BF16),
             v((512, 256), F32),
@@ -527,8 +561,7 @@
             v((16, 2, 16, 128), BF16),
             v((8, 2, 2, 16, 128), F32),
             v((8, 2, 2, 16, 128), F32),
-            v((4, 1, 256), F32),
-            v((8, 1, 256), F32),
+            v((32, 1, 256), F32),
             v((128, 128), F32),
             v((128, 128), F32),
             v((4, 128, 128), F32),

time: 86.1 us -> 82.3 us (0.956)
  Pallas kernels: 84.7 us -> 80.7 us
    pallas_call x1, Pallas kernels: 83.6 us -> 79.6 us  [on_device(): pl.pallas_call(kernel, out_shape=outs, in_specs=[hb] * 9 + [pl.BlockSpec(...]
where the time goes in v3:
time: 82.3 us; the launch traced here: 82.1 us
  Pallas kernels  80.7 us (98%)
  between operations  1.45 us (2%)
    pallas_call x1, Pallas kernels, on_device(): pl.pallas_call(kernel, out_shape=outs, in_specs=[hb] * 9 + [pl.BlockSpec(...  79.6 us

profile of v3, /device:TPU:1, one launch (start us, length us, event | category | flops | bytes accessed | tf_op | source)
XLA Modules:
  0.0 82.1 jit_solution(8281979808774565894)
XLA Ops:
  1.3 79.6 %shard_map.172 = (bf16[256,1024]{1,0:T(8,128)(2,1)S(1)}, bf16[2,256,128]{2,1,0:T(8,128)(2,1)S(1)}, f32[2,2,16,128]{3,2,1,0:T(8,128)S(1)}, bf16[512,128]{1,0:T(8,...) custom-call(bf16[256,1024]{1,0:T(8,128)(2,1)} %q_hbm.1, bf16[256,128]{1,0:T(8,128)(2,1)} %sk_hbm.1, ...), custom_call_target="tpu_custom_call" | custom-call | tf_op jit(solution)/shard_map/pallas_call | solution.py:526
  80.9 1.1 %shard_map.173 = (bf16[256,1024]{1,0:T(8,128)(2,1)}, bf16[2,256,128]{2,1,0:T(8,128)(2,1)}, f32[2,2,16,128]{3,2,1,0:T(8,128)}, bf16[512,128]{1,0:T(8,128)(2,1)}, f32[512,128]{1,0:T(8,128)}, /*index=5*/f32[128,256]{1,0:T(8,128)}) custom-call(bf16[256,1024]{1,0:T(8,128)(2,1)S(1)} %get-tuple-element.12.refs_0_, ...), custom_call_target="tpu_custom_call" | custom-call | tf_op jit(solution)/shard_map/pallas_call | solution.py:578
